TPU v7x, 32 devices: a whole 2x2x4 slice. The times are simulated.
32 devices in a mesh: chan: 16 (over z, x, core), tm: 2 (over y).
Axes of the slice: x: 2, y: 2, z: 4, core: 2. Of those that a mesh axis runs over, the one named last changes fastest.
Arguments:
- samples: bfloat16 [96, 2, 2048], P('chan', 'tm'), may hold values from -6 to 6
- dead_flags: int32 [96], P('chan'), may hold values 0 or 1
- pair_mask: int32 [96, 96], P('chan', 'tm'), may hold values 0 or 1
Outputs:
- xcorr: float32 [96, 96, 301], P('chan', 'tm')
All inputs are finite; a program needn't handle non-finite values. No bound on the sum of `dead_flags` or of `pair_mask` on one device may be relied on, other than what follows from the above.
Results may differ from a plain program's by a relative error of at most 0.0095.
Values may be sent and summed in bfloat16 or wider, within the bound.
A program may use at most 64 MiB of HBM per device.

v0:
```python
import math

import jax
import jax.numpy as jnp
from jax import lax
from jax.sharding import PartitionSpec as P

F = 768
LAGS = 301


def taper_window(length):
    sample_index = jnp.arange(length, dtype=jnp.float32)
    return 0.5 - 0.5 * jnp.cos(2.0 * math.pi * (sample_index + 0.5) / length)


def forward_table(length, bins):
    sample_index = jnp.arange(length, dtype=jnp.int32)
    frequency = jnp.arange(1, bins + 1, dtype=jnp.int32)
    phase_index = sample_index[:, None] * frequency[None, :] % length
    angles = 2.0 * math.pi / length * phase_index.astype(jnp.float32)
    return jnp.concatenate([jnp.cos(angles), -jnp.sin(angles)], axis=1).astype(jnp.bfloat16)


def lag_table(length, bins, lags, factor):
    frequency = jnp.arange(1, bins + 1, dtype=jnp.int32)
    shifts = jnp.arange(lags, dtype=jnp.int32) - (lags - 1) // 2
    phase_index = jnp.mod(frequency[:, None] * shifts[None, :], length)
    angles = 2.0 * math.pi / length * phase_index.astype(jnp.float32)
    table_values = jnp.concatenate([jnp.cos(angles), -jnp.sin(angles)], axis=0) * factor
    return table_values.astype(jnp.bfloat16)


def whiten(samples, dead_flags, table_values):
    channel_count, windows, length = samples.shape
    bins = table_values.shape[1] // 2
    traces = samples.astype(jnp.float32)
    traces = traces - jnp.mean(traces, axis=-1, keepdims=True)
    tapered = (traces * taper_window(length)).astype(jnp.bfloat16)
    spectra = jnp.dot(
        tapered.reshape(channel_count * windows, length),
        table_values,
        preferred_element_type=jnp.float32,
    )
    real_part = spectra[:, :bins]
    imag_part = spectra[:, bins:]
    energy = real_part * real_part + imag_part * imag_part
    mean_energy = jnp.mean(energy, axis=-1, keepdims=True)
    inverse_scale = lax.rsqrt(energy + 0.25 * mean_energy + 1e-06)
    alive_rows = jnp.repeat((1 - dead_flags).astype(jnp.float32), windows)[:, None]
    whitened = (
        jnp.concatenate([real_part * inverse_scale, imag_part * inverse_scale], axis=1) * alive_rows
    )
    return whitened.astype(jnp.bfloat16).reshape(channel_count, windows, 2 * bins)


def correlate(receivers, sources, lag_weights):
    bins = receivers.shape[-1] // 2
    rec_values = receivers.astype(jnp.float32)
    src_values = sources.astype(jnp.float32)
    rec_re = rec_values[:, None, :, :bins]
    rec_im = rec_values[:, None, :, bins:]
    src_re = src_values[None, :, :, :bins]
    src_im = src_values[None, :, :, bins:]
    cross_re = rec_re * src_re + rec_im * src_im
    cross_im = rec_im * src_re - rec_re * src_im
    cross = jnp.concatenate([cross_re, cross_im], axis=-1).astype(jnp.bfloat16)
    result = jnp.einsum("rgwk,kl->wrgl", cross, lag_weights, preferred_element_type=jnp.float32)
    return result.astype(jnp.bfloat16)


def pick_group(source_count, rows_each):
    chosen = 1
    for candidate in range(1, source_count + 1):
        if source_count % candidate == 0 and candidate * rows_each <= 1024:
            chosen = candidate
    return chosen


def per_device(samples, dead_flags, pair_mask):
    block_size, local_windows, length = samples.shape
    table_values = forward_table(length, F)
    whitened = whiten(samples, dead_flags, table_values)
    subwin = local_windows * lax.axis_size("tm")
    lag_weights = lag_table(length, F, LAGS, 1.0 / math.sqrt(subwin * F))
    incoming = lax.all_gather(whitened, "chan", axis=0, tiled=True)
    source_count = incoming.shape[0]
    group_size = pick_group(source_count, block_size * local_windows)
    grouped = incoming.reshape(source_count // group_size, group_size, local_windows, 2 * F)

    def one_group(group_sources):
        return correlate(whitened, group_sources, lag_weights)[0]

    results = lax.map(one_group, grouped)
    placed = jnp.transpose(results, (1, 0, 2, 3)).reshape(block_size, source_count, LAGS)
    shares = lax.psum_scatter(
        placed.astype(jnp.float32).astype(jnp.bfloat16), "tm", scatter_dimension=1, tiled=True
    ).astype(jnp.float32)
    return shares * pair_mask.astype(jnp.float32)[..., None]


def solution(mesh):
    in_specs = (P("chan", "tm", None), P("chan"), P("chan", "tm"))
    out_specs = P("chan", "tm", None)
    return jax.shard_map(
        per_device, mesh=mesh, in_specs=in_specs, out_specs=out_specs, check_vma=False
    )
```

profile of v0, /device:TPU:0, one launch (start us, length us, event | category | flops | bytes accessed | tf_op | source)
XLA Modules:
  0.0 85.0 jit_solution(8352473777845611654)
XLA Ops:
  6.5 0.0 reduce-scatter.2.cloned.1.call-start
  6.5 0.1 multiply_subtract_fusion
  6.6 0.0 copy-start
  6.6 25.4 %cosine_convert_fusion = (bf16[2048,768]{1,0:T(8,128)(2,1)S(1)}, bf16[2048,768]{1,0:T(8,128)(2,1)S(1)}) fusion(s32[768]{0:T(1024)S(1)} %iota_add_fusion), kind=kLoop, calls=%fused_computation.11 | loop fusion | flops 26738688 | bytes 6294528 | tf_op jit(solution)/shard_map/convert.2
  32.1 0.0 copy-done
  32.1 0.1 convert_reduce_fusion
  32.2 0.0 copy-start.2
  32.2 1.0 %fusion.3 = f32[6,1536]{1,0:T(8,128)S(1)} fusion(bf16[2048,768]{1,0:T(8,128)(2,1)S(1)} %get-tuple-element.33, bf16[2048,768]{1,0:T(8,128)(2,1)S(1)} %get-tuple-element.32, bf16[6,1,2048]{2,0,1:T(8,128)(2,1)S(1)} %copy-done, f32[2048]{0:T(1024)S(1)} %multiply_subtract_fusion, f32[6]{0:T(128)S(1)} %broadcast_multiply_fusion.1), kind=kOutput, calls=%fused_computation.6 | convolution fusion | flops 50380800 | bytes 6361112 | tf_op jit(solution)/shard_map/dot_general | solution.py:40
  33.2 0.1 fusion.39
  33.3 0.1 multiply_bitcast_fusion.1
  33.4 0.0 copy-done.2
  33.4 0.1 fusion.40
  33.5 24.9 %all_gather.3 = bf16[96,1,1536]{2,1,0:T(2,128)(2,1)S(1)} all-gather(bf16[6,1,1536]{2,1,0:T(2,128)(2,1)S(1)} %copy.4), channel_id=1, replica_groups=mesh['chan'=16,'tm'=2] {'chan'}, dimensions={0}, use_global_device_ids=true | all-gather | bytes 313344 | tf_op jit(solution)/shard_map/all_gather | solution.py:86
  58.4 0.6 fusion.42
  59.0 3.7 %fusion.27 = (f32[768,301]{0,1:T(8,128)S(1)}, f32[768,301]{0,1:T(8,128)S(1)}) fusion(s32[301]{0:T(512)S(1)} %iota_add_fusion.1, s32[768]{0:T(1024)S(1)} %iota_add_fusion), kind=kLoop, calls=%fused_computation.36 | loop fusion | flops 3467520 | bytes 1853620 | tf_op jit(solution)/shard_map/cos | solution.py:30
  62.8 0.5 add_convert_fusion
  63.3 0.0 copy-start.1
  63.3 1.9 %fusion.18 = bf16[6,96,301]{2,1,0:T(8,128)(2,1)} fusion(bf16[6,96,768]{2,1,0:T(8,128)(2,1)S(1)} %get-tuple-element.22, bf16[6,96,768]{2,1,0:T(8,128)(2,1)S(1)} %get-tuple-element.20, f32[768,301]{0,1:T(8,128)S(1)} %get-tuple-element.31, f32[768,301]{0,1:T(8,128)S(1)} %get-tuple-element.30), kind=kOutput, calls=%fused_computation.29 | convolution fusion | flops 537710400 | bytes 3965568 | tf_op jit(solution)/shard_map/while/body/eval_jaxpr/rgwk,kl->wrgl/dot_general | solution.py:68
  65.2 0.0 reduce-scatter.2.cloned.1.call-update
  65.2 0.0 copy-done.1
  65.2 11.2 %reduce-scatter.2.cloned.1.call-done = bf16[6,48,301]{2,1,0:T(8,128)(2,1)} async-done(((bf16[6,96,301]{2,1,0:T(8,128)(2,1)}), bf16[6,48,301]{2,1,0:T(8,128)(2,1)}) %reduce-scatter.2.cloned.1.call-update) | async-done | bytes 173392 | tf_op jit(solution)/shard_map/reduce_scatter | solution.py:96
  76.4 1.8 %convert_multiply_fusion = f32[6,48,301]{2,1,0:T(8,128)} fusion(bf16[6,48,301]{2,1,0:T(8,128)(2,1)} %reduce-scatter.2.cloned.1.call-done, f32[6,48]{1,0:T(8,128)S(1)} %convert_element_type.91), kind=kLoop, calls=%fused_computation.37 | loop fusion | flops 173376 | bytes 521280 | tf_op jit(solution)/shard_map/mul | solution.py:99
  (9 shorter events, 0.1 us)
Async XLA Ops:
  6.5 69.9 %reduce-scatter.2.cloned.1.call-start = ((), (), s32[]{:S(2)}) async-start(), calls=%async_computation.1 | async-start | bytes 663552 | tf_op jit(solution)/shard_map/reduce_scatter | solution.py:96
  6.6 25.5 %copy-start = (bf16[6,1,2048]{2,0,1:T(8,128)(2,1)S(1)}, bf16[6,1,2048]{2,0,1:T(8,128)(2,1)}, u32[]{:S(2)}) copy-start(bf16[6,1,2048]{2,0,1:T(8,128)(2,1)} %param.3) | copy-start | bytes 73732
  32.2 1.2 %copy-start.2 = (s32[6]{0:T(128)S(1)}, s32[6]{0:T(128)}, u32[]{:S(2)}) copy-start(s32[6]{0:T(128)} %param.4) | copy-start | bytes 76
  63.3 1.9 %copy-start.1 = (s32[6,48]{1,0:T(8,128)S(1)}, s32[6,48]{1,0:T(8,128)}, u32[]{:S(2)}) copy-start(s32[6,48]{1,0:T(8,128)} %param.5) | copy-start | bytes 3460
Sparse Core Ops, SparseCore 0:
  65.3 11.0 reduce-scatter.1
where the time goes:
time: 85.2 us; the launch traced here: 85 us
  other arithmetic  32 us (38%)
  blocking collectives  24.9 us (29%)
  between operations  13.5 us (16%)
  waiting for transfers between devices  11.2 us (13%)
  matrix products  2.82 us (3%)
    another operation x2, other arithmetic  25.9 us
    all_gather x1, blocking collectives, per_device(): incoming = lax.all_gather(whitened, 'chan', axis=0, tiled=True)  24.9 us
    reduce_scatter x1, waiting for transfers between devices, per_device(): lax.psum_scatter(placed.astype(jnp.float32).astype(jnp.bfloat16), 'tm', s...  11.2 us
    cos x1, other arithmetic, lag_table(): jnp.cos(angles)  3.74 us
    dot_general x1, matrix products, correlate(): jnp.einsum('rgwk,kl->wrgl', cross, lag_weights, preferred_element_type=jn...  1.86 us
    mul x1, other arithmetic, per_device(): return shares * pair_mask.astype(jnp.float32)[..., None]  1.8 us
  transfers between devices with their start and end apart: 1, of which 1 were waited for; matrix products, arithmetic and copies ran while one was open for 0% of the time, Pallas kernels for 0%

commit v1 on v0

--- a/solution.py
+++ b/solution.py
@@ -1,8 +1,12 @@
+import functools
 import math
 
 import jax
 import jax.numpy as jnp
+import numpy as np
 from jax import lax
+from jax.experimental import pallas as pl
+from jax.experimental.pallas import tpu as pltpu
 from jax.sharding import PartitionSpec as P
 
 F = 768
@@ -99,9 +103,292 @@
     return shares * pair_mask.astype(jnp.float32)[..., None]
 
 
+RADIX = 16
+LANES = 128
+MESH = pl.DeviceIdType.MESH
+
+
+def frequency_groups(bins):
+    half = RADIX // 2
+    groups = []
+    for residue in range(half):
+        first, second = (0, half) if residue == 0 else (residue, RADIX - residue)
+        all_bins = np.arange(1, bins + 1)
+        groups.append((first, second, all_bins[all_bins % RADIX == first], all_bins[all_bins % RADIX == second]))
+    return groups
+
+
+def split_tables(length, bins):
+    depth = length // RADIX
+    offsets = np.arange(depth)
+    columns_re, columns_im, owner, order = [], [], [], []
+    for index, (first, second, bins_a, bins_b) in enumerate(frequency_groups(bins)):
+        for which, chosen in ((0, bins_a), (1, bins_b)):
+            for k in chosen:
+                angle = 2.0 * np.pi / length * ((offsets * k) % length)
+                cos, sin, zero = np.cos(angle), np.sin(angle), np.zeros(depth)
+                if index == 0:
+                    re = [cos, zero] if which == 0 else [zero, cos]
+                    im = [-sin, zero] if which == 0 else [zero, -sin]
+                elif which == 0:
+                    re, im = [cos, sin], [-sin, cos]
+                else:
+                    re, im = [cos, -sin], [-sin, -cos]
+                columns_re.append(np.concatenate(re))
+                columns_im.append(np.concatenate(im))
+                owner.append(index)
+                order.append(k)
+    tiles = bins // LANES
+    table = np.zeros((tiles, 4 * depth, 2 * LANES), np.float32)
+    reads = []
+    for tile in range(tiles):
+        owners = sorted(set(owner[tile * LANES : (tile + 1) * LANES]))
+        assert len(owners) <= 2
+        reads.append(tuple(owners))
+        for lane in range(LANES):
+            at = tile * LANES + lane
+            base = owners.index(owner[at]) * 2 * depth
+            table[tile, base : base + 2 * depth, lane] = columns_re[at]
+            table[tile, base : base + 2 * depth, LANES + lane] = columns_im[at]
+    return table, reads, np.array(order)
+
+
+def ordered_lag_table(length, order, lags, factor):
+    shifts = np.arange(lags) - (lags - 1) // 2
+    angles = 2.0 * np.pi / length * np.mod(order[:, None] * shifts[None, :], length)
+    values = np.concatenate([np.cos(angles), -np.sin(angles)], axis=0) * factor
+    padded = -(-lags // LANES) * LANES
+    return np.pad(values, ((0, 0), (0, padded - lags))).astype(np.float32)
+
+
+def stage_one(pieces):
+    half = RADIX // 2
+    sums = [pieces[a] + pieces[RADIX - a] for a in range(1, half)]
+    diffs = [pieces[a] - pieces[RADIX - a] for a in range(1, half)]
+    even = pieces[0] + pieces[half]
+    odd = pieces[0] - pieces[half]
+
+    def real(k):
+        total = even if k % 2 == 0 else odd
+        for a in range(1, half):
+            total = total + sums[a - 1] * float(np.cos(2 * np.pi * a * k / RADIX))
+        return total
+
+    def imag(k):
+        total = diffs[0] * float(-np.sin(2 * np.pi * k / RADIX))
+        for a in range(2, half):
+            total = total + diffs[a - 1] * float(-np.sin(2 * np.pi * a * k / RADIX))
+        return total
+
+    groups = [jnp.concatenate([real(0), real(half)], axis=1)]
+    for k in range(1, half):
+        groups.append(jnp.concatenate([real(k), imag(k)], axis=1))
+    return [g.astype(jnp.bfloat16) for g in groups]
+
+
+def fused_kernel(
+    sizes, reads, samples_ref, dead_ref, taper_ref, table_ref, lag_ref, out_ref,
+    own, src, rec, srcf, cross, table, lagv,
+    table_sem, send_sem, pair_sem, fwd_sem, src_sem, rec_sem,
+):
+    chans, tms, block, group, bins = sizes
+    me_c, me_t = lax.axis_index("chan"), lax.axis_index("tm")
+    core = me_c % 2
+    columns = chans // 2
+    load_table = pltpu.make_async_copy(table_ref, table, table_sem.at[0])
+    load_table.start()
+    load_lag = pltpu.make_async_copy(lag_ref, lagv, table_sem.at[1])
+    load_lag.start()
+
+    barrier = pltpu.get_barrier_semaphore()
+    everyone = columns * tms
+    flat = (me_c // 2) * tms + me_t
+    for step in range(1, everyone):
+        other = (flat + step) % everyone
+        pl.semaphore_signal(
+            barrier, inc=1, device_id=((other // tms) * 2 + core, other % tms), device_id_type=MESH
+        )
+    sibling = me_c + 1 - 2 * core
+    pl.semaphore_signal(barrier, inc=1, device_id=(sibling, me_t), device_id_type=MESH)
+
+    length = samples_ref.shape[-1]
+    depth = length // RADIX
+    traces = samples_ref[...].reshape(block, length).astype(jnp.float32)
+    traces = traces - jnp.mean(traces, axis=-1, keepdims=True)
+    tapered = (traces * taper_ref[...]).astype(jnp.bfloat16).astype(jnp.float32)
+    groups = stage_one([tapered[:, a * depth : (a + 1) * depth] for a in range(RADIX)])
+    row = lax.broadcasted_iota(jnp.int32, (block, 1), 0)
+    alive = jnp.zeros((block, 1), jnp.float32)
+    for r in range(block):
+        alive = jnp.where(row == r, (1 - dead_ref[r]).astype(jnp.float32), alive)
+    load_table.wait()
+    parts = []
+    energy_sum = jnp.zeros((block, LANES), jnp.float32)
+    for tile, owners in enumerate(reads):
+        lhs = jnp.concatenate([groups[g] for g in owners], axis=1)
+        spec = jnp.dot(lhs, table[tile, : lhs.shape[1], :], preferred_element_type=jnp.float32)
+        re, im = spec[:, :LANES], spec[:, LANES:]
+        energy = re * re + im * im
+        energy_sum = energy_sum + energy
+        parts.append((re, im, energy))
+    mean_energy = jnp.sum(energy_sum, axis=-1, keepdims=True) / bins
+    for tile, (re, im, energy) in enumerate(parts):
+        scale = lax.rsqrt(energy + 0.25 * mean_energy + 1e-06)
+        lanes = slice(tile * LANES, (tile + 1) * LANES)
+        lanes_im = slice(bins + tile * LANES, bins + (tile + 1) * LANES)
+        own[:, lanes] = (re * scale * alive).astype(jnp.bfloat16)
+        own[:, lanes_im] = (im * scale * alive).astype(jnp.bfloat16)
+
+    pl.semaphore_wait(barrier, everyone)
+
+    to_t = me_c // group
+    slot = me_c % group
+
+    def push(column):
+        to_c = 2 * column + core
+        return pltpu.make_async_remote_copy(
+            src_ref=own, dst_ref=src.at[slot, me_t],
+            send_sem=send_sem.at[column], recv_sem=src_sem.at[slot, me_t],
+            device_id=(to_c, to_t), device_id_type=MESH,
+        )
+
+    for column in range(columns):
+        is_self = jnp.logical_and(2 * column + core == me_c, to_t == me_t)
+
+        @pl.when(jnp.logical_not(is_self))
+        def _():
+            push(column).start()
+
+        @pl.when(is_self)
+        def _():
+            pltpu.make_async_copy(own, src.at[slot, me_t], src_sem.at[slot, me_t]).start()
+
+    def pair_copy(step):
+        return pltpu.make_async_remote_copy(
+            src_ref=own, dst_ref=rec.at[me_t],
+            send_sem=pair_sem.at[step], recv_sem=rec_sem.at[me_t],
+            device_id=(me_c, (me_t + step) % tms), device_id_type=MESH,
+        )
+
+    for step in range(1, tms):
+        pair_copy(step).start()
+    own_rec = pltpu.make_async_copy(own, rec.at[me_t], pair_sem.at[0])
+    own_rec.start()
+
+    def arrival(b, w):
+        return pltpu.make_async_copy(own, src.at[b, w], src_sem.at[b, w])
+
+    def forward(b, w):
+        return pltpu.make_async_remote_copy(
+            src_ref=src.at[b, w], dst_ref=src.at[b, w],
+            send_sem=fwd_sem.at[b, w], recv_sem=src_sem.at[b, w],
+            device_id=(sibling, me_t), device_id_type=MESH,
+        )
+
+    for half_block in range(group // 2):
+        for w in range(tms):
+            b = 2 * half_block + core
+            arrival(b, w).wait()
+            forward(b, w).start()
+    own_rec.wait()
+    for step in range(1, tms):
+        from_t = (me_t + step) % tms
+        pltpu.make_async_copy(own, rec.at[from_t], rec_sem.at[from_t]).wait()
+    for half_block in range(group // 2):
+        for w in range(tms):
+            arrival(2 * half_block + 1 - core, w).wait()
+
+    sources = group * block
+    for b in range(group):
+        for w in range(tms):
+            srcf[w, b * block : (b + 1) * block, :] = src[b, w].astype(jnp.float32)
+    for tile in range(bins // LANES):
+        lanes = slice(tile * LANES, (tile + 1) * LANES)
+        lanes_im = slice(bins + tile * LANES, bins + (tile + 1) * LANES)
+        rec_re = [rec[w, :, lanes].astype(jnp.float32) for w in range(tms)]
+        rec_im = [rec[w, :, lanes_im].astype(jnp.float32) for w in range(tms)]
+        src_re = [srcf[w, :, lanes] for w in range(tms)]
+        src_im = [srcf[w, :, lanes_im] for w in range(tms)]
+        for r in range(block):
+            total_re = total_im = None
+            for w in range(tms):
+                a, c = rec_re[w][r : r + 1, :], rec_im[w][r : r + 1, :]
+                now_re = a * src_re[w] + c * src_im[w]
+                now_im = c * src_re[w] - a * src_im[w]
+                total_re = now_re if total_re is None else total_re + now_re
+                total_im = now_im if total_im is None else total_im + now_im
+            cross[r * sources : (r + 1) * sources, lanes] = total_re.astype(jnp.bfloat16)
+            cross[r * sources : (r + 1) * sources, lanes_im] = total_im.astype(jnp.bfloat16)
+    load_lag.wait()
+    lags = out_ref.shape[-1]
+    for r in range(block):
+        result = jnp.dot(
+            cross[r * sources : (r + 1) * sources, :], lagv[...], preferred_element_type=jnp.float32
+        )
+        out_ref[r] = result[:, :lags]
+
+    for column in range(columns):
+        is_self = jnp.logical_and(2 * column + core == me_c, to_t == me_t)
+
+        @pl.when(jnp.logical_not(is_self))
+        def _():
+            push(column).wait_send()
+
+    for step in range(1, tms):
+        pair_copy(step).wait_send()
+    for half_block in range(group // 2):
+        for w in range(tms):
+            forward(2 * half_block + core, w).wait_send()
+
+
+def fused_device(chans, tms, samples, dead_flags, pair_mask):
+    block, _, length = samples.shape
+    sources = pair_mask.shape[1]
+    group = sources // block
+    table, reads, order = split_tables(length, F)
+    lag_weights = ordered_lag_table(length, order, LAGS, 1.0 / math.sqrt(tms * F))
+    at = np.arange(length)
+    taper = (0.5 - 0.5 * np.cos(2.0 * np.pi * (at + 0.5) / length))[None, :].astype(np.float32)
+    vmem, hbm = pl.BlockSpec(memory_space=pltpu.VMEM), pl.BlockSpec(memory_space=pl.ANY)
+    sem = pltpu.SemaphoreType.DMA
+    result = pl.pallas_call(
+        functools.partial(fused_kernel, (chans, tms, block, group, F), reads),
+        out_shape=jax.ShapeDtypeStruct((block, sources, LAGS), jnp.float32),
+        in_specs=[vmem, pl.BlockSpec(memory_space=pltpu.SMEM), vmem, hbm, hbm],
+        out_specs=vmem,
+        scratch_shapes=[
+            pltpu.VMEM((block, 2 * F), jnp.bfloat16),
+            pltpu.VMEM((group, tms, block, 2 * F), jnp.bfloat16),
+            pltpu.VMEM((tms, block, 2 * F), jnp.bfloat16),
+            pltpu.VMEM((tms, sources, 2 * F), jnp.float32),
+            pltpu.VMEM((block * sources, 2 * F), jnp.bfloat16),
+            pltpu.VMEM(table.shape, jnp.bfloat16),
+            pltpu.VMEM(lag_weights.shape, jnp.bfloat16),
+            sem((2,)), sem((chans // 2,)), sem((tms,)), sem((group, tms)), sem((group, tms)), sem((tms,)),
+        ],
+        compiler_params=pltpu.CompilerParams(collective_id=0, has_side_effects=True),
+    )(
+        samples, dead_flags, jnp.asarray(taper),
+        jnp.asarray(table, jnp.bfloat16), jnp.asarray(lag_weights, jnp.bfloat16),
+    )
+    return result * pair_mask.astype(jnp.float32)[..., None]
+
+
+def dispatch(chans, tms, samples, dead_flags, pair_mask):
+    block, windows, length = samples.shape
+    sources = pair_mask.shape[1]
+    whole_blocks = sources % (2 * block) == 0 and chans % 2 == 0 and sources % 16 == 0
+    aligned = length == RADIX * LANES and F % LANES == 0 and windows == 1
+    if whole_blocks and aligned:
+        return fused_device(chans, tms, samples, dead_flags, pair_mask)
+    return per_device(samples, dead_flags, pair_mask)
+
+
 def solution(mesh):
     in_specs = (P("chan", "tm", None), P("chan"), P("chan", "tm"))
     out_specs = P("chan", "tm", None)
+    chans, tms = mesh.shape["chan"], mesh.shape["tm"]
     return jax.shard_map(
-        per_device, mesh=mesh, in_specs=in_specs, out_specs=out_specs, check_vma=False
+        functools.partial(dispatch, chans, tms),
+        mesh=mesh, in_specs=in_specs, out_specs=out_specs, check_vma=False,
     )

time: 85.2 us -> 18.9 us (0.22)
  the two profiles are of different devices: /device:TPU:0 before, /device:TPU:7 now
where the time goes in v1:
time: 18.9 us; the launch traced here: 18.6 us
  Pallas kernels  15.3 us (81%)
  other arithmetic  1.89 us (10%)
  local copies, waits for them, and re-layouts  1.42 us (8%)
    pallas_call x1, Pallas kernels, fused_device(): pl.pallas_call(functools.partial(fused_kernel, (chans, tms, block, group,...  15.3 us
    mul x1, other arithmetic, fused_device(): return result * pair_mask.astype(jnp.float32)[..., None]  1.88 us
    unnamed x3, local copies, waits for them, and re-layouts  1.42 us

profile of v1, /device:TPU:7, one launch (start us, length us, event | category | flops | bytes accessed | tf_op | source)
XLA Modules:
  0.0 18.6 jit_solution(11712020275091298946)
XLA Ops:
  0.0 1.4 %copy.7.samples_ref = bf16[6,1,2048]{2,1,0:T(2,128)(2,1)} copy(bf16[6,1,2048]{2,0,1:T(8,128)(2,1)} %param.6) | data formatting | bytes 49152 | tf_op args[0]
  1.4 0.0 copy-start
  1.4 15.3 %shard_map.64 = f32[6,48,301]{2,1,0:T(8,128)} custom-call(bf16[6,1,2048]{2,1,0:T(2,128)(2,1)} %copy.7.samples_ref, s32[6]{0:T(128)} %dead_ref.1, f32[1,2048]{1,0:T(1,128)} %constant.6.clone.taper_ref, bf16[6,512,256]{2,1,0:T(8,128)(2,1)} %constant.7.clone.table_ref, bf16[1536,384]{1,0:T(8,128)(2,1)} %constant.8.clone.lag_ref), custom_call_target="tpu_custom_call" | custom-call | tf_op jit(solution)/shard_map/pallas_call | solution.py:354
  16.7 0.0 copy-done
  16.7 1.9 %broadcast_multiply_fusion = f32[6,48,301]{2,1,0:T(8,128)} fusion(f32[6,48,301]{2,1,0:T(8,128)} %shard_map.64, f32[6,48]{1,0:T(8,128)S(1)} %convert_element_type.3), kind=kLoop, calls=%fused_computation | loop fusion | flops 86688 | bytes 694656 | tf_op jit(solution)/shard_map/mul | solution.py:374
  (1 shorter events, 0.0 us)
Async XLA Ops:
  1.4 15.3 %copy-start = (s32[6,48]{1,0:T(8,128)S(1)}, s32[6,48]{1,0:T(8,128)}, u32[]{:S(2)}) copy-start(s32[6,48]{1,0:T(8,128)} %param.8) | copy-start | bytes 3460

commit v2 on v1

--- a/solution.py
+++ b/solution.py
@@ -187,14 +187,20 @@
 
 
 def fused_kernel(
-    sizes, reads, samples_ref, dead_ref, taper_ref, table_ref, lag_ref, out_ref,
-    own, src, rec, srcf, cross, table, lagv,
-    table_sem, send_sem, pair_sem, fwd_sem, src_sem, rec_sem,
+    sizes, reads, samples_hbm, dead_hbm, taper_hbm, table_ref, lag_ref, out_ref,
+    samples_ref, dead_ref, taper_ref, own, src, rec, srcf, cross, table, lagv,
+    outv, table_sem, send_sem, pair_sem, fwd_sem, src_sem, rec_sem, out_sem,
 ):
     chans, tms, block, group, bins = sizes
     me_c, me_t = lax.axis_index("chan"), lax.axis_index("tm")
     core = me_c % 2
     columns = chans // 2
+    load_samples = pltpu.make_async_copy(samples_hbm, samples_ref, table_sem.at[2])
+    load_samples.start()
+    load_dead = pltpu.make_async_copy(dead_hbm, dead_ref, table_sem.at[4])
+    load_dead.start()
+    load_taper = pltpu.make_async_copy(taper_hbm, taper_ref, table_sem.at[3])
+    load_taper.start()
     load_table = pltpu.make_async_copy(table_ref, table, table_sem.at[0])
     load_table.start()
     load_lag = pltpu.make_async_copy(lag_ref, lagv, table_sem.at[1])
@@ -213,10 +219,13 @@
 
     length = samples_ref.shape[-1]
     depth = length // RADIX
-    traces = samples_ref[...].reshape(block, length).astype(jnp.float32)
+    load_samples.wait()
+    load_taper.wait()
+    traces = samples_ref[...].astype(jnp.float32)
     traces = traces - jnp.mean(traces, axis=-1, keepdims=True)
     tapered = (traces * taper_ref[...]).astype(jnp.bfloat16).astype(jnp.float32)
     groups = stage_one([tapered[:, a * depth : (a + 1) * depth] for a in range(RADIX)])
+    load_dead.wait()
     row = lax.broadcasted_iota(jnp.int32, (block, 1), 0)
     alive = jnp.zeros((block, 1), jnp.float32)
     for r in range(block):
@@ -325,8 +334,11 @@
         result = jnp.dot(
             cross[r * sources : (r + 1) * sources, :], lagv[...], preferred_element_type=jnp.float32
         )
-        out_ref[r] = result[:, :lags]
-
+        outv[r] = result[:, :lags]
+        pltpu.make_async_copy(outv.at[r], out_ref.at[r], out_sem.at[r]).start()
+
+    for r in range(block):
+        pltpu.make_async_copy(outv.at[r], out_ref.at[r], out_sem.at[r]).wait()
     for column in range(columns):
         is_self = jnp.logical_and(2 * column + core == me_c, to_t == me_t)
 
@@ -349,14 +361,17 @@
     lag_weights = ordered_lag_table(length, order, LAGS, 1.0 / math.sqrt(tms * F))
     at = np.arange(length)
     taper = (0.5 - 0.5 * np.cos(2.0 * np.pi * (at + 0.5) / length))[None, :].astype(np.float32)
-    vmem, hbm = pl.BlockSpec(memory_space=pltpu.VMEM), pl.BlockSpec(memory_space=pl.ANY)
+    anywhere, hbm = pl.BlockSpec(memory_space=pl.ANY), pl.BlockSpec(memory_space=pltpu.HBM)
     sem = pltpu.SemaphoreType.DMA
     result = pl.pallas_call(
         functools.partial(fused_kernel, (chans, tms, block, group, F), reads),
         out_shape=jax.ShapeDtypeStruct((block, sources, LAGS), jnp.float32),
-        in_specs=[vmem, pl.BlockSpec(memory_space=pltpu.SMEM), vmem, hbm, hbm],
-        out_specs=vmem,
+        in_specs=[hbm] * 5,
+        out_specs=anywhere,
         scratch_shapes=[
+            pltpu.VMEM((block, length), jnp.bfloat16),
+            pltpu.SMEM((block,), jnp.int32),
+            pltpu.VMEM((1, length), jnp.float32),
             pltpu.VMEM((block, 2 * F), jnp.bfloat16),
             pltpu.VMEM((group, tms, block, 2 * F), jnp.bfloat16),
             pltpu.VMEM((tms, block, 2 * F), jnp.bfloat16),
@@ -364,12 +379,18 @@
             pltpu.VMEM((block * sources, 2 * F), jnp.bfloat16),
             pltpu.VMEM(table.shape, jnp.bfloat16),
             pltpu.VMEM(lag_weights.shape, jnp.bfloat16),
-            sem((2,)), sem((chans // 2,)), sem((tms,)), sem((group, tms)), sem((group, tms)), sem((tms,)),
+            pltpu.VMEM((block, sources, LAGS), jnp.float32),
+            sem((5,)), sem((chans // 2,)), sem((tms,)), sem((group, tms)), sem((group, tms)), sem((tms,)), sem((block,)),
         ],
-        compiler_params=pltpu.CompilerParams(collective_id=0, has_side_effects=True),
+        compiler_params=pltpu.CompilerParams(collective_id=0, has_side_effects=True, vmem_limit_bytes=24 * 1024 * 1024),
     )(
-        samples, dead_flags, jnp.asarray(taper),
-        jnp.asarray(table, jnp.bfloat16), jnp.asarray(lag_weights, jnp.bfloat16),
+        *(
+            pltpu.with_memory_space_constraint(operand, pltpu.HBM)
+            for operand in (
+                samples.reshape(block, length), dead_flags, jnp.asarray(taper),
+                jnp.asarray(table, jnp.bfloat16), jnp.asarray(lag_weights, jnp.bfloat16),
+            )
+        )
     )
     return result * pair_mask.astype(jnp.float32)[..., None]
 

time: 18.9 us -> 16.6 us (0.88)
  the two profiles are of different devices: /device:TPU:7 before, /device:TPU:5 now
where the time goes in v2:
time: 16.6 us; the launch traced here: 16.4 us
  Pallas kernels  14.9 us (90%)
  other arithmetic  1.56 us (9%)
    pallas_call x1, Pallas kernels, fused_device(): pl.pallas_call(functools.partial(fused_kernel, (chans, tms, block, group,...  14.9 us
    mul x1, other arithmetic, fused_device(): return result * pair_mask.astype(jnp.float32)[..., None]  0.87 us
    convert_element_type x1, other arithmetic, fused_device(): return result * pair_mask.astype(jnp.float32)[..., None]  0.69 us

profile of v2, /device:TPU:5, one launch (start us, length us, event | category | flops | bytes accessed | tf_op | source)
XLA Modules:
  0.0 16.4 jit_solution(15326089357467787721)
XLA Ops:
  0.0 0.7 %convert_element_type.3 = f32[6,48]{1,0:T(8,128)S(1)} convert(s32[6,48]{1,0:T(8,128)} %param.8) | non-fusion elementwise | flops 288 | bytes 2304 | tf_op jit(solution)/shard_map/convert_element_type | solution.py:395
  0.7 14.9 %shard_map.64 = f32[6,48,301]{2,1,0:T(8,128)S(1)} custom-call(bf16[6,2048]{1,0:T(8,128)(2,1)} %bitcast.1, s32[6]{0:T(128)} %dead_hbm.1, f32[1,2048]{1,0:T(1,128)} %constant.6.clone.taper_hbm, bf16[6,512,256]{2,1,0:T(8,128)(2,1)} %constant.7.clone.table_ref, bf16[1536,384]{1,0:T(8,128)(2,1)} %constant.8.clone.lag_ref), custom_call_target="tpu_custom_call" | custom-call | tf_op jit(solution)/shard_map/pallas_call | solution.py:366
  15.6 0.9 %broadcast_multiply_fusion = f32[6,48,301]{2,1,0:T(8,128)} fusion(f32[6,48,301]{2,1,0:T(8,128)S(1)} %shard_map.64, f32[6,48]{1,0:T(8,128)S(1)} %convert_element_type.3), kind=kLoop, calls=%fused_computation | loop fusion | flops 86688 | bytes 694656 | tf_op jit(solution)/shard_map/mul | solution.py:395

commit v3 on v2

--- a/solution.py
+++ b/solution.py
@@ -187,9 +187,9 @@
 
 
 def fused_kernel(
-    sizes, reads, samples_hbm, dead_hbm, taper_hbm, table_ref, lag_ref, out_ref,
-    samples_ref, dead_ref, taper_ref, own, src, rec, srcf, cross, table, lagv,
-    outv, table_sem, send_sem, pair_sem, fwd_sem, src_sem, rec_sem, out_sem,
+    sizes, reads, samples_hbm, dead_hbm, mask_hbm, taper_hbm, table_ref, lag_ref, out_ref, keep_ref,
+    samples_ref, dead_ref, maskv, taper_ref, own, src, rec, srcf, cross, table, lagv,
+    table_sem, send_sem, pair_sem, fwd_sem, src_sem, rec_sem,
 ):
     chans, tms, block, group, bins = sizes
     me_c, me_t = lax.axis_index("chan"), lax.axis_index("tm")
@@ -199,6 +199,8 @@
     load_samples.start()
     load_dead = pltpu.make_async_copy(dead_hbm, dead_ref, table_sem.at[4])
     load_dead.start()
+    load_mask = pltpu.make_async_copy(mask_hbm, maskv, table_sem.at[5])
+    load_mask.start()
     load_taper = pltpu.make_async_copy(taper_hbm, taper_ref, table_sem.at[3])
     load_taper.start()
     load_table = pltpu.make_async_copy(table_ref, table, table_sem.at[0])
@@ -207,14 +209,20 @@
     load_lag.start()
 
     barrier = pltpu.get_barrier_semaphore()
-    everyone = columns * tms
-    flat = (me_c // 2) * tms + me_t
-    for step in range(1, everyone):
-        other = (flat + step) % everyone
+    sibling = me_c + 1 - 2 * core
+    half = group // 2
+    for i in range(half):
+        for w in range(tms):
+            from_c = me_t * group + core * half + i
+
+            @pl.when(jnp.logical_not(jnp.logical_and(from_c == me_c, w == me_t)))
+            def _():
+                pl.semaphore_signal(barrier, inc=1, device_id=(from_c, w), device_id_type=MESH)
+
+    for step in range(1, tms):
         pl.semaphore_signal(
-            barrier, inc=1, device_id=((other // tms) * 2 + core, other % tms), device_id_type=MESH
+            barrier, inc=1, device_id=(me_c, (me_t + step) % tms), device_id_type=MESH
         )
-    sibling = me_c + 1 - 2 * core
     pl.semaphore_signal(barrier, inc=1, device_id=(sibling, me_t), device_id_type=MESH)
 
     length = samples_ref.shape[-1]
@@ -248,29 +256,34 @@
         own[:, lanes] = (re * scale * alive).astype(jnp.bfloat16)
         own[:, lanes_im] = (im * scale * alive).astype(jnp.bfloat16)
 
-    pl.semaphore_wait(barrier, everyone)
-
     to_t = me_c // group
     slot = me_c % group
-
-    def push(column):
-        to_c = 2 * column + core
+    to_half, at = slot // half, slot % half
+    keeps = jnp.logical_and(to_t == me_t, to_half == core)
+    pl.semaphore_wait(barrier, columns + tms - keeps.astype(jnp.int32))
+
+    def column_at(i):
+        return (me_c // 2 + columns // 2 + i) % columns
+
+    def stays(i):
+        return jnp.logical_and(keeps, column_at(i) == me_c // 2)
+
+    def push(i):
         return pltpu.make_async_remote_copy(
-            src_ref=own, dst_ref=src.at[slot, me_t],
-            send_sem=send_sem.at[column], recv_sem=src_sem.at[slot, me_t],
-            device_id=(to_c, to_t), device_id_type=MESH,
+            src_ref=own, dst_ref=src.at[to_half, at, me_t],
+            send_sem=send_sem.at[i], recv_sem=src_sem.at[to_half, at, me_t],
+            device_id=(2 * column_at(i) + to_half, to_t), device_id_type=MESH,
         )
 
-    for column in range(columns):
-        is_self = jnp.logical_and(2 * column + core == me_c, to_t == me_t)
-
-        @pl.when(jnp.logical_not(is_self))
+    for i in range(columns):
+
+        @pl.when(jnp.logical_not(stays(i)))
         def _():
-            push(column).start()
-
-        @pl.when(is_self)
+            push(i).start()
+
+        @pl.when(stays(i))
         def _():
-            pltpu.make_async_copy(own, src.at[slot, me_t], src_sem.at[slot, me_t]).start()
+            pltpu.make_async_copy(own, src.at[to_half, at, me_t], src_sem.at[to_half, at, me_t]).start()
 
     def pair_copy(step):
         return pltpu.make_async_remote_copy(
@@ -284,73 +297,79 @@
     own_rec = pltpu.make_async_copy(own, rec.at[me_t], pair_sem.at[0])
     own_rec.start()
 
-    def arrival(b, w):
-        return pltpu.make_async_copy(own, src.at[b, w], src_sem.at[b, w])
-
-    def forward(b, w):
+    def arrival(h, i, w):
+        return pltpu.make_async_copy(own, src.at[h, i, w], src_sem.at[h, i, w])
+
+    def forward(i, w):
         return pltpu.make_async_remote_copy(
-            src_ref=src.at[b, w], dst_ref=src.at[b, w],
-            send_sem=fwd_sem.at[b, w], recv_sem=src_sem.at[b, w],
+            src_ref=src.at[core, i, w], dst_ref=src.at[core, i, w],
+            send_sem=fwd_sem.at[i, w], recv_sem=src_sem.at[core, i, w],
             device_id=(sibling, me_t), device_id_type=MESH,
         )
 
-    for half_block in range(group // 2):
+    sources = half * block
+    lags = out_ref.shape[-1]
+
+    def correlate_half(h):
+        for i in range(half):
+            for w in range(tms):
+                srcf[w, i * block : (i + 1) * block, :] = src[h, i, w].astype(jnp.float32)
+        for tile in range(bins // LANES):
+            lanes = slice(tile * LANES, (tile + 1) * LANES)
+            lanes_im = slice(bins + tile * LANES, bins + (tile + 1) * LANES)
+            rec_re = [rec[w, :, lanes].astype(jnp.float32) for w in range(tms)]
+            rec_im = [rec[w, :, lanes_im].astype(jnp.float32) for w in range(tms)]
+            src_re = [srcf[w, :, lanes] for w in range(tms)]
+            src_im = [srcf[w, :, lanes_im] for w in range(tms)]
+            for r in range(block):
+                total_re = total_im = None
+                for w in range(tms):
+                    a, c = rec_re[w][r : r + 1, :], rec_im[w][r : r + 1, :]
+                    now_re = a * src_re[w] + c * src_im[w]
+                    now_im = c * src_re[w] - a * src_im[w]
+                    total_re = now_re if total_re is None else total_re + now_re
+                    total_im = now_im if total_im is None else total_im + now_im
+                cross[r * sources : (r + 1) * sources, lanes] = total_re.astype(jnp.bfloat16)
+                cross[r * sources : (r + 1) * sources, lanes_im] = total_im.astype(jnp.bfloat16)
+        result = jnp.dot(cross[...], lagv[...], preferred_element_type=jnp.float32)
+        for r in range(block):
+            out_ref[r, pl.ds(pl.multiple_of(h * sources, sources), sources), :] = result[
+                r * sources : (r + 1) * sources, :lags
+            ]
+
+    for i in range(half):
         for w in range(tms):
-            b = 2 * half_block + core
-            arrival(b, w).wait()
-            forward(b, w).start()
+            arrival(core, i, w).wait()
+            forward(i, w).start()
+    load_mask.wait()
+    keep_ref[...] = maskv[...].astype(jnp.float32)
+    load_lag.wait()
     own_rec.wait()
     for step in range(1, tms):
         from_t = (me_t + step) % tms
         pltpu.make_async_copy(own, rec.at[from_t], rec_sem.at[from_t]).wait()
-    for half_block in range(group // 2):
-        for w in range(tms):
-            arrival(2 * half_block + 1 - core, w).wait()
-
-    sources = group * block
-    for b in range(group):
-        for w in range(tms):
-            srcf[w, b * block : (b + 1) * block, :] = src[b, w].astype(jnp.float32)
-    for tile in range(bins // LANES):
-        lanes = slice(tile * LANES, (tile + 1) * LANES)
-        lanes_im = slice(bins + tile * LANES, bins + (tile + 1) * LANES)
-        rec_re = [rec[w, :, lanes].astype(jnp.float32) for w in range(tms)]
-        rec_im = [rec[w, :, lanes_im].astype(jnp.float32) for w in range(tms)]
-        src_re = [srcf[w, :, lanes] for w in range(tms)]
-        src_im = [srcf[w, :, lanes_im] for w in range(tms)]
-        for r in range(block):
-            total_re = total_im = None
-            for w in range(tms):
-                a, c = rec_re[w][r : r + 1, :], rec_im[w][r : r + 1, :]
-                now_re = a * src_re[w] + c * src_im[w]
-                now_im = c * src_re[w] - a * src_im[w]
-                total_re = now_re if total_re is None else total_re + now_re
-                total_im = now_im if total_im is None else total_im + now_im
-            cross[r * sources : (r + 1) * sources, lanes] = total_re.astype(jnp.bfloat16)
-            cross[r * sources : (r + 1) * sources, lanes_im] = total_im.astype(jnp.bfloat16)
-    load_lag.wait()
-    lags = out_ref.shape[-1]
-    for r in range(block):
-        result = jnp.dot(
-            cross[r * sources : (r + 1) * sources, :], lagv[...], preferred_element_type=jnp.float32
-        )
-        outv[r] = result[:, :lags]
-        pltpu.make_async_copy(outv.at[r], out_ref.at[r], out_sem.at[r]).start()
-
-    for r in range(block):
-        pltpu.make_async_copy(outv.at[r], out_ref.at[r], out_sem.at[r]).wait()
-    for column in range(columns):
-        is_self = jnp.logical_and(2 * column + core == me_c, to_t == me_t)
-
-        @pl.when(jnp.logical_not(is_self))
+
+    @pl.loop(0, 2)
+    def _(turn):
+        @pl.when(turn == 1)
         def _():
-            push(column).wait_send()
+            for i in range(half):
+                for w in range(tms):
+                    arrival(1 - core, i, w).wait()
+
+        correlate_half((core + turn) % 2)
+
+    for i in range(columns):
+
+        @pl.when(jnp.logical_not(stays(i)))
+        def _():
+            push(i).wait_send()
 
     for step in range(1, tms):
         pair_copy(step).wait_send()
-    for half_block in range(group // 2):
+    for i in range(half):
         for w in range(tms):
-            forward(2 * half_block + core, w).wait_send()
+            forward(i, w).wait_send()
 
 
 def fused_device(chans, tms, samples, dead_flags, pair_mask):
@@ -361,44 +380,50 @@
     lag_weights = ordered_lag_table(length, order, LAGS, 1.0 / math.sqrt(tms * F))
     at = np.arange(length)
     taper = (0.5 - 0.5 * np.cos(2.0 * np.pi * (at + 0.5) / length))[None, :].astype(np.float32)
-    anywhere, hbm = pl.BlockSpec(memory_space=pl.ANY), pl.BlockSpec(memory_space=pltpu.HBM)
+    vmem, hbm = pl.BlockSpec(memory_space=pltpu.VMEM), pl.BlockSpec(memory_space=pltpu.HBM)
     sem = pltpu.SemaphoreType.DMA
-    result = pl.pallas_call(
+    half = group // 2
+    result, keep = pl.pallas_call(
         functools.partial(fused_kernel, (chans, tms, block, group, F), reads),
-        out_shape=jax.ShapeDtypeStruct((block, sources, LAGS), jnp.float32),
-        in_specs=[hbm] * 5,
-        out_specs=anywhere,
+        out_shape=[
+            pltpu.VMEM((block, sources, LAGS), jnp.float32),
+            pltpu.VMEM((block, sources), jnp.float32),
+        ],
+        in_specs=[hbm] * 6,
+        out_specs=[vmem] * 2,
         scratch_shapes=[
             pltpu.VMEM((block, length), jnp.bfloat16),
             pltpu.SMEM((block,), jnp.int32),
+            pltpu.VMEM((block, sources), jnp.int32),
             pltpu.VMEM((1, length), jnp.float32),
             pltpu.VMEM((block, 2 * F), jnp.bfloat16),
-            pltpu.VMEM((group, tms, block, 2 * F), jnp.bfloat16),
+            pltpu.VMEM((2, half, tms, block, 2 * F), jnp.bfloat16),
             pltpu.VMEM((tms, block, 2 * F), jnp.bfloat16),
-            pltpu.VMEM((tms, sources, 2 * F), jnp.float32),
-            pltpu.VMEM((block * sources, 2 * F), jnp.bfloat16),
+            pltpu.VMEM((tms, half * block, 2 * F), jnp.float32),
+            pltpu.VMEM((block * half * block, 2 * F), jnp.bfloat16),
             pltpu.VMEM(table.shape, jnp.bfloat16),
             pltpu.VMEM(lag_weights.shape, jnp.bfloat16),
-            pltpu.VMEM((block, sources, LAGS), jnp.float32),
-            sem((5,)), sem((chans // 2,)), sem((tms,)), sem((group, tms)), sem((group, tms)), sem((tms,)), sem((block,)),
+            sem((6,)), sem((chans // 2,)), sem((tms,)), sem((half, tms)), sem((2, half, tms)), sem((tms,)),
         ],
-        compiler_params=pltpu.CompilerParams(collective_id=0, has_side_effects=True, vmem_limit_bytes=24 * 1024 * 1024),
+        compiler_params=pltpu.CompilerParams(
+            collective_id=0, has_side_effects=True, vmem_limit_bytes=24 * 1024 * 1024
+        ),
     )(
         *(
             pltpu.with_memory_space_constraint(operand, pltpu.HBM)
             for operand in (
-                samples.reshape(block, length), dead_flags, jnp.asarray(taper),
+                samples.reshape(block, length), dead_flags, pair_mask, jnp.asarray(taper),
                 jnp.asarray(table, jnp.bfloat16), jnp.asarray(lag_weights, jnp.bfloat16),
             )
         )
     )
-    return result * pair_mask.astype(jnp.float32)[..., None]
+    return result * keep[..., None]
 
 
 def dispatch(chans, tms, samples, dead_flags, pair_mask):
     block, windows, length = samples.shape
     sources = pair_mask.shape[1]
-    whole_blocks = sources % (2 * block) == 0 and chans % 2 == 0 and sources % 16 == 0
+    whole_blocks = sources % (2 * block) == 0 and chans % 2 == 0 and sources % 16 == 0 and block * chans == sources * tms
     aligned = length == RADIX * LANES and F % LANES == 0 and windows == 1
     if whole_blocks and aligned:
         return fused_device(chans, tms, samples, dead_flags, pair_mask)

time: 16.6 us -> 14.7 us (0.89)
  Pallas kernels: 14.9 us -> 13.6 us
  other arithmetic: 1.56 us -> 0.87 us
    pallas_call x1, Pallas kernels: 14.9 us -> 13.6 us  [fused_device(): pl.pallas_call(functools.partial(fused_kernel, (chans, tms, block, group,...]
    convert_element_type x1 -> x0, other arithmetic: 0.69 us -> none  [fused_device(): return result * pair_mask.astype(jnp.float32)[..., None]]
where the time goes in v3:
time: 14.7 us; the launch traced here: 14.5 us
  Pallas kernels  13.6 us (93%)
  other arithmetic  0.87 us (6%)
    pallas_call x1, Pallas kernels, fused_device(): pl.pallas_call(functools.partial(fused_kernel, (chans, tms, block, group,...  13.6 us
    mul x1, other arithmetic, fused_device(): return result * keep[..., None]  0.87 us

profile of v3, /device:TPU:5, one launch (start us, length us, event | category | flops | bytes accessed | tf_op | source)
XLA Modules:
  0.0 14.5 jit_solution(18172772977272150272)
XLA Ops:
  0.0 13.6 %shard_map.64 = (f32[6,48,301]{2,1,0:T(8,128)S(1)}, f32[6,48]{1,0:T(8,128)S(1)}) custom-call(bf16[6,2048]{1,0:T(8,128)(2,1)} %bitcast.1, s32[6]{0:T(128)} %dead_hbm.1, s32[6,48]{1,0:T(8,128)} %mask_hbm.1, f32[1,2048]{1,0:T(1,128)} %constant.6.clone.taper_hbm, bf16[6,512,256]{2,1,0:T(8,128)(2,1)} %constant.7.clone.table_ref, ...), custom_call_target="tpu_custom_call" | custom-call | tf_op jit(solution)/shard_map/pallas_call | solution.py:386
  13.6 0.9 %broadcast_multiply_fusion = f32[6,48,301]{2,1,0:T(8,128)} fusion(f32[6,48,301]{2,1,0:T(8,128)S(1)} %get-tuple-element.7, f32[6,48]{1,0:T(8,128)S(1)} %get-tuple-element.8), kind=kLoop, calls=%fused_computation | loop fusion | flops 86688 | bytes 694656 | tf_op jit(solution)/shard_map/mul | solution.py:420

commit v4 on v3

--- a/solution.py
+++ b/solution.py
@@ -105,6 +105,7 @@
 
 RADIX = 16
 LANES = 128
+ROWS = 8
 MESH = pl.DeviceIdType.MESH
 
 
@@ -161,6 +162,18 @@
     return np.pad(values, ((0, 0), (0, padded - lags))).astype(np.float32)
 
 
+def packing(block, length):
+    width = block * length // ROWS
+    tail = length - width
+    return width, tail, width // tail if tail > 0 else 0
+
+
+def packs(block, length):
+    width, tail, chunks = packing(block, length)
+    full = block < ROWS and block * length % (ROWS * LANES) == 0
+    return full and tail % LANES == 0 and width % tail == 0 and (ROWS - block) * chunks == block
+
+
 def stage_one(pieces):
     half = RADIX // 2
     sums = [pieces[a] + pieces[RADIX - a] for a in range(1, half)]
@@ -188,13 +201,30 @@
 
 def fused_kernel(
     sizes, reads, samples_hbm, dead_hbm, mask_hbm, taper_hbm, table_ref, lag_ref, out_ref, keep_ref,
-    samples_ref, dead_ref, maskv, taper_ref, own, src, rec, srcf, cross, table, lagv,
+    samples_ref, dead_ref, maskv, taper_ref, packed, own, src, rec, recf, srcf, cross, table, lagv,
     table_sem, send_sem, pair_sem, fwd_sem, src_sem, rec_sem,
 ):
     chans, tms, block, group, bins = sizes
     me_c, me_t = lax.axis_index("chan"), lax.axis_index("tm")
     core = me_c % 2
     columns = chans // 2
+    barrier = pltpu.get_barrier_semaphore()
+    sibling = me_c + 1 - 2 * core
+    half = group // 2
+    for i in range(half):
+        for w in range(tms):
+            from_c = me_t * group + core * half + i
+
+            @pl.when(jnp.logical_not(jnp.logical_and(from_c == me_c, w == me_t)))
+            def _():
+                pl.semaphore_signal(barrier, inc=1, device_id=(from_c, w), device_id_type=MESH)
+
+    for step in range(1, tms):
+        pl.semaphore_signal(
+            barrier, inc=1, device_id=(me_c, (me_t + step) % tms), device_id_type=MESH
+        )
+    pl.semaphore_signal(barrier, inc=1, device_id=(sibling, me_t), device_id_type=MESH)
+
     load_samples = pltpu.make_async_copy(samples_hbm, samples_ref, table_sem.at[2])
     load_samples.start()
     load_dead = pltpu.make_async_copy(dead_hbm, dead_ref, table_sem.at[4])
@@ -207,23 +237,6 @@
     load_table.start()
     load_lag = pltpu.make_async_copy(lag_ref, lagv, table_sem.at[1])
     load_lag.start()
-
-    barrier = pltpu.get_barrier_semaphore()
-    sibling = me_c + 1 - 2 * core
-    half = group // 2
-    for i in range(half):
-        for w in range(tms):
-            from_c = me_t * group + core * half + i
-
-            @pl.when(jnp.logical_not(jnp.logical_and(from_c == me_c, w == me_t)))
-            def _():
-                pl.semaphore_signal(barrier, inc=1, device_id=(from_c, w), device_id_type=MESH)
-
-    for step in range(1, tms):
-        pl.semaphore_signal(
-            barrier, inc=1, device_id=(me_c, (me_t + step) % tms), device_id_type=MESH
-        )
-    pl.semaphore_signal(barrier, inc=1, device_id=(sibling, me_t), device_id_type=MESH)
 
     length = samples_ref.shape[-1]
     depth = length // RADIX
@@ -248,13 +261,31 @@
         energy = re * re + im * im
         energy_sum = energy_sum + energy
         parts.append((re, im, energy))
+    width, tail, chunks = packing(block, 2 * bins)
+
+    def pack(start, piece):
+        if start < width:
+            packed[:block, start : start + LANES] = piece
+            return
+        for r in range(block):
+            first = (r % chunks) * tail + start - width
+            packed[block + r // chunks : block + r // chunks + 1, first : first + LANES] = piece[r : r + 1]
+
+    def unpack(values, store):
+        store(slice(0, block), slice(0, width), values[:block])
+        for r in range(block):
+            first = (r % chunks) * tail
+            store(
+                slice(r, r + 1), slice(width, width + tail),
+                values[block + r // chunks : block + r // chunks + 1, first : first + tail],
+            )
+
     mean_energy = jnp.sum(energy_sum, axis=-1, keepdims=True) / bins
     for tile, (re, im, energy) in enumerate(parts):
         scale = lax.rsqrt(energy + 0.25 * mean_energy + 1e-06)
-        lanes = slice(tile * LANES, (tile + 1) * LANES)
-        lanes_im = slice(bins + tile * LANES, bins + (tile + 1) * LANES)
-        own[:, lanes] = (re * scale * alive).astype(jnp.bfloat16)
-        own[:, lanes_im] = (im * scale * alive).astype(jnp.bfloat16)
+        pack(tile * LANES, re * scale * alive)
+        pack(bins + tile * LANES, im * scale * alive)
+    own[...] = packed[...].astype(jnp.bfloat16)
 
     to_t = me_c // group
     slot = me_c % group
@@ -313,12 +344,16 @@
     def correlate_half(h):
         for i in range(half):
             for w in range(tms):
-                srcf[w, i * block : (i + 1) * block, :] = src[h, i, w].astype(jnp.float32)
+
+                def store(rows, lanes, piece):
+                    srcf[w, i * block + rows.start : i * block + rows.stop, lanes] = piece
+
+                unpack(src[h, i, w].astype(jnp.float32), store)
         for tile in range(bins // LANES):
             lanes = slice(tile * LANES, (tile + 1) * LANES)
             lanes_im = slice(bins + tile * LANES, bins + (tile + 1) * LANES)
-            rec_re = [rec[w, :, lanes].astype(jnp.float32) for w in range(tms)]
-            rec_im = [rec[w, :, lanes_im].astype(jnp.float32) for w in range(tms)]
+            rec_re = [recf[w, :, lanes] for w in range(tms)]
+            rec_im = [recf[w, :, lanes_im] for w in range(tms)]
             src_re = [srcf[w, :, lanes] for w in range(tms)]
             src_im = [srcf[w, :, lanes_im] for w in range(tms)]
             for r in range(block):
@@ -349,6 +384,13 @@
         from_t = (me_t + step) % tms
         pltpu.make_async_copy(own, rec.at[from_t], rec_sem.at[from_t]).wait()
 
+    for w in range(tms):
+
+        def store_rec(rows, lanes, piece):
+            recf[w, rows, lanes] = piece
+
+        unpack(rec[w].astype(jnp.float32), store_rec)
+
     @pl.loop(0, 2)
     def _(turn):
         @pl.when(turn == 1)
@@ -383,6 +425,7 @@
     vmem, hbm = pl.BlockSpec(memory_space=pltpu.VMEM), pl.BlockSpec(memory_space=pltpu.HBM)
     sem = pltpu.SemaphoreType.DMA
     half = group // 2
+    width = packing(block, 2 * F)[0]
     result, keep = pl.pallas_call(
         functools.partial(fused_kernel, (chans, tms, block, group, F), reads),
         out_shape=[
@@ -396,9 +439,11 @@
             pltpu.SMEM((block,), jnp.int32),
             pltpu.VMEM((block, sources), jnp.int32),
             pltpu.VMEM((1, length), jnp.float32),
-            pltpu.VMEM((block, 2 * F), jnp.bfloat16),
-            pltpu.VMEM((2, half, tms, block, 2 * F), jnp.bfloat16),
-            pltpu.VMEM((tms, block, 2 * F), jnp.bfloat16),
+            pltpu.VMEM((ROWS, width), jnp.float32),
+            pltpu.VMEM((ROWS, width), jnp.bfloat16),
+            pltpu.VMEM((2, half, tms, ROWS, width), jnp.bfloat16),
+            pltpu.VMEM((tms, ROWS, width), jnp.bfloat16),
+            pltpu.VMEM((tms, block, 2 * F), jnp.float32),
             pltpu.VMEM((tms, half * block, 2 * F), jnp.float32),
             pltpu.VMEM((block * half * block, 2 * F), jnp.bfloat16),
             pltpu.VMEM(table.shape, jnp.bfloat16),
@@ -425,7 +470,7 @@
     sources = pair_mask.shape[1]
     whole_blocks = sources % (2 * block) == 0 and chans % 2 == 0 and sources % 16 == 0 and block * chans == sources * tms
     aligned = length == RADIX * LANES and F % LANES == 0 and windows == 1
-    if whole_blocks and aligned:
+    if whole_blocks and aligned and packs(block, 2 * F):
         return fused_device(chans, tms, samples, dead_flags, pair_mask)
     return per_device(samples, dead_flags, pair_mask)
 

time: 14.7 us -> 13.5 us (0.918)
  Pallas kernels: 13.6 us -> 12.5 us
    pallas_call x1, Pallas kernels: 13.6 us -> 12.5 us  [fused_device(): pl.pallas_call(functools.partial(fused_kernel, (chans, tms, block, group,...]
where the time goes in v4:
time: 13.5 us; the launch traced here: 13.4 us
  Pallas kernels  12.5 us (93%)
  other arithmetic  0.87 us (6%)
    pallas_call x1, Pallas kernels, fused_device(): pl.pallas_call(functools.partial(fused_kernel, (chans, tms, block, group,...  12.5 us
    mul x1, other arithmetic, fused_device(): return result * keep[..., None]  0.87 us

profile of v4, /device:TPU:5, one launch (start us, length us, event | category | flops | bytes accessed | tf_op | source)
XLA Modules:
  0.0 13.4 jit_solution(2614458316036103902)
XLA Ops:
  0.0 12.5 %shard_map.64 = (f32[6,48,301]{2,1,0:T(8,128)S(1)}, f32[6,48]{1,0:T(8,128)S(1)}) custom-call(bf16[6,2048]{1,0:T(8,128)(2,1)} %bitcast.1, s32[6]{0:T(128)} %dead_hbm.1, s32[6,48]{1,0:T(8,128)} %mask_hbm.1, f32[1,2048]{1,0:T(1,128)} %constant.6.clone.taper_hbm, bf16[6,512,256]{2,1,0:T(8,128)(2,1)} %constant.7.clone.table_ref, ...), custom_call_target="tpu_custom_call" | custom-call | tf_op jit(solution)/shard_map/pallas_call | solution.py:429
  12.5 0.9 %broadcast_multiply_fusion = f32[6,48,301]{2,1,0:T(8,128)} fusion(f32[6,48,301]{2,1,0:T(8,128)S(1)} %get-tuple-element.7, f32[6,48]{1,0:T(8,128)S(1)} %get-tuple-element.8), kind=kLoop, calls=%fused_computation | loop fusion | flops 86688 | bytes 694656 | tf_op jit(solution)/shard_map/mul | solution.py:465

commit v5 on v4

--- a/solution.py
+++ b/solution.py
@@ -294,7 +294,7 @@
     pl.semaphore_wait(barrier, columns + tms - keeps.astype(jnp.int32))
 
     def column_at(i):
-        return (me_c // 2 + columns // 2 + i) % columns
+        return (me_c // 2 + i) % columns
 
     def stays(i):
         return jnp.logical_and(keeps, column_at(i) == me_c // 2)

time: 13.5 us -> 12.6 us (0.933)
  Pallas kernels: 12.5 us -> 11.5 us
    pallas_call x1, Pallas kernels: 12.5 us -> 11.5 us  [fused_device(): pl.pallas_call(functools.partial(fused_kernel, (chans, tms, block, group,...]
where the time goes in v5:
time: 12.6 us; the launch traced here: 12.4 us
  Pallas kernels  11.5 us (91%)
  other arithmetic  0.87 us (7%)
    pallas_call x1, Pallas kernels, fused_device(): pl.pallas_call(functools.partial(fused_kernel, (chans, tms, block, group,...  11.5 us
    mul x1, other arithmetic, fused_device(): return result * keep[..., None]  0.87 us

profile of v5, /device:TPU:5, one launch (start us, length us, event | category | flops | bytes accessed | tf_op | source)
XLA Modules:
  0.0 12.4 jit_solution(6873729582832867091)
XLA Ops:
  0.0 11.5 %shard_map.64 = (f32[6,48,301]{2,1,0:T(8,128)S(1)}, f32[6,48]{1,0:T(8,128)S(1)}) custom-call(bf16[6,2048]{1,0:T(8,128)(2,1)} %bitcast.1, s32[6]{0:T(128)} %dead_hbm.1, s32[6,48]{1,0:T(8,128)} %mask_hbm.1, f32[1,2048]{1,0:T(1,128)} %constant.6.clone.taper_hbm, bf16[6,512,256]{2,1,0:T(8,128)(2,1)} %constant.7.clone.table_ref, ...), custom_call_target="tpu_custom_call" | custom-call | tf_op jit(solution)/shard_map/pallas_call | solution.py:429
  11.6 0.9 %broadcast_multiply_fusion = f32[6,48,301]{2,1,0:T(8,128)} fusion(f32[6,48,301]{2,1,0:T(8,128)S(1)} %get-tuple-element.7, f32[6,48]{1,0:T(8,128)S(1)} %get-tuple-element.8), kind=kLoop, calls=%fused_computation | loop fusion | flops 86688 | bytes 694656 | tf_op jit(solution)/shard_map/mul | solution.py:465
